TPU v7x, 512 devices: a whole 4x8x8 slice. The times are simulated.
512 devices in a mesh: depth: 16 (over z, core), rows: 32 (over y, x).
Axes of the slice: x: 4, y: 8, z: 8, core: 2. Of those that a mesh axis runs over, the one named last changes fastest.
Arguments:
- in_flight: float32 [16, 2, 1024, 1024], P('depth', None, 'rows'), may hold values from -6 to 6
- phase_index: bfloat16 [32, 1024, 1024], P('depth', 'rows'), may hold values from -2 to 2
- absorption: bfloat16 [32, 1024, 1024], P('depth', 'rows'), may hold values from 0.099609375 to 2
Outputs:
- exits: float32 [16, 2, 1024, 1024], P('depth', None, 'rows')
All inputs are finite; a program needn't handle non-finite values.
Results may differ from a plain program's by a relative error of at most 0.0003.
Values may be sent and summed in bfloat16 or wider, within the bound.
A program may use at most 64 MiB of HBM per device.

v0:
```python
import functools
import math

import jax
import jax.numpy as jnp
import ml_dtypes
import numpy as np
from jax import lax
from jax.experimental import pallas as pl
from jax.experimental.pallas import tpu as pltpu
from jax.sharding import PartitionSpec as P

TAYLOR = 4
SLICES = 2
HALO = 8
LANES = 128
lateral = 0.22
contrast = 0.2
MESH = pl.DeviceIdType.MESH


def middle_matrices(length):
    coarse = length // LANES
    b = np.arange(LANES)
    k = np.arange(length)
    f = np.where(k < length // 2, k, k - length)
    gain = np.exp(-1j * np.pi * ((f * f) % (8 * length)) / (4 * length))
    dft = np.exp(-2j * np.pi * (np.outer(b, b) % LANES) / LANES)
    whole = np.zeros((coarse, 2 * LANES, 2 * LANES))
    for k1 in range(coarse):
        twiddle = np.exp(-2j * np.pi * b * k1 / length)
        m = (twiddle[:, None] * dft * gain[k1 + coarse * b][None, :]) @ (np.conj(dft) * np.conj(twiddle)[None, :])
        m = m / length
        whole[k1] = np.block([[m.real, m.imag], [-m.imag, m.real]])
    high = whole.astype(np.float32).astype(ml_dtypes.bfloat16)
    low = (whole - high.astype(np.float64)).astype(np.float32).astype(ml_dtypes.bfloat16)
    return high, low


def radix8(re, im, sign):
    half = math.sqrt(0.5)

    def turn(r, i):
        return (-i, r) if sign > 0 else (i, -r)

    def four(r, i):
        a, b = (r[0] + r[2], i[0] + i[2]), (r[0] - r[2], i[0] - i[2])
        c, d = (r[1] + r[3], i[1] + i[3]), (r[1] - r[3], i[1] - i[3])
        d = turn(*d)
        return [(a[0] + c[0], a[1] + c[1]), (b[0] + d[0], b[1] + d[1]), (a[0] - c[0], a[1] - c[1]), (b[0] - d[0], b[1] - d[1])]

    even = four(re[0::2], im[0::2])
    odd = four(re[1::2], im[1::2])
    s = 1.0 if sign > 0 else -1.0
    o1, o3 = odd[1], odd[3]
    odd[1] = ((o1[0] - s * o1[1]) * half, (o1[1] + s * o1[0]) * half)
    odd[2] = turn(*odd[2])
    odd[3] = ((-o3[0] - s * o3[1]) * half, (-o3[1] + s * o3[0]) * half)
    out = [(e[0] + o[0], e[1] + o[1]) for e, o in zip(even, odd)]
    out += [(e[0] - o[0], e[1] - o[1]) for e, o in zip(even, odd)]
    return [v[0] for v in out], [v[1] for v in out]


def swap_quarters(vs, lane):
    low64 = lane < 64
    low32 = lax.rem(lane, 64) < 32

    def roll(x, by):
        return pltpu.roll(x, by, 1)

    a0 = jnp.where(low64, vs[0], roll(vs[2], 64))
    a2 = jnp.where(low64, roll(vs[0], 64), vs[2])
    a1 = jnp.where(low64, vs[1], roll(vs[3], 64))
    a3 = jnp.where(low64, roll(vs[1], 64), vs[3])
    return [
        jnp.where(low32, a0, roll(a1, 32)),
        jnp.where(low32, roll(a0, 96), a1),
        jnp.where(low32, a2, roll(a3, 32)),
        jnp.where(low32, roll(a2, 96), a3),
    ]


def kernel(
    groups, rows, field_ref, index_ref, loss_ref, high_hbm, low_hbm, out_ref,
    high_ref, low_ref, term, total, coef, damp, edge, lhs, mid, field_halo, spec_send, spec_halo,
    b_send, b_recv, c_send, c_recv, d_send, d_recv,
    load_sem, halo_send_sem, halo_recv_sem, b_sems, c_sems, d_sems,
):
    depth = lax.axis_index("depth")
    me = lax.axis_index("rows")
    ahead = lax.rem(depth + 1, groups)
    behind = lax.rem(depth + groups - 1, groups)
    right, left = lax.rem(me + 1, rows), lax.rem(me + rows - 1, rows)
    tiles = high_ref.shape[0]
    slab = field_ref.shape[2]
    tall = slab + 2 * HALO

    loads = [
        pltpu.make_async_copy(high_hbm, high_ref, load_sem.at[0]),
        pltpu.make_async_copy(low_hbm, low_ref, load_sem.at[1]),
    ]
    for load in loads:
        load.start()

    barrier = pltpu.get_barrier_semaphore()

    def greet(step, carry):
        pl.semaphore_signal(barrier, inc=1, device_id=(depth, lax.rem(me + step, rows)), device_id_type=MESH)
        return carry

    def greet_behind(step, carry):
        pl.semaphore_signal(barrier, inc=1, device_id=(behind, lax.rem(me + step, rows)), device_id_type=MESH)
        return carry

    lax.fori_loop(1, rows, greet, 0)
    lax.fori_loop(0, rows, greet_behind, 0)

    lane32 = lax.broadcasted_iota(jnp.int32, (32, LANES), 1)
    lane16 = lax.broadcasted_iota(jnp.int32, (16, LANES), 1)
    lane_tall = lax.broadcasted_iota(jnp.int32, (tall, LANES), 1)
    row_tall = lax.broadcasted_iota(jnp.int32, (tall, LANES), 0)
    outside = ((row_tall < HALO) & (me == 0)) | ((row_tall >= HALO + slab) & (me == rows - 1))
    lat = jnp.where(outside, 0.0, lateral)
    first_lane = lane_tall == 0
    last_lane = lane_tall == LANES - 1
    lat_slab = jnp.full((slab, LANES), lateral, jnp.float32)

    for slot in range(2):
        for part in range(2):
            for a in range(tiles):
                term[slot, part, a, 0:HALO] = jnp.zeros((HALO, LANES), jnp.float32)
                term[slot, part, a, tall + HALO : tall + 2 * HALO] = jnp.zeros((HALO, LANES), jnp.float32)

    def all_copies(src, dst, sems, to_depth, step):
        target = lax.rem(me + step, rows)
        return pltpu.make_async_remote_copy(
            src_ref=src.at[target], dst_ref=dst.at[me], send_sem=sems.at[0, step], recv_sem=sems.at[1, step],
            device_id=(to_depth, target), device_id_type=MESH,
        )

    def start_all(src, dst, sems, to_depth, first):
        def body(step, carry):
            all_copies(src, dst, sems, to_depth, step).start()
            return carry

        lax.fori_loop(first, rows, body, 0)

    def wait_recv_all(src, dst, sems, to_depth, first):
        def body(step, carry):
            source = lax.rem(me + rows - step, rows)
            pltpu.make_async_remote_copy(
                src_ref=src.at[source], dst_ref=dst.at[source], send_sem=sems.at[0, step], recv_sem=sems.at[1, step],
                device_id=(to_depth, source), device_id_type=MESH,
            ).wait_recv()
            return carry

        lax.fori_loop(first, rows, body, 0)

    def wait_send_all(src, dst, sems, to_depth, first):
        def body(step, carry):
            all_copies(src, dst, sems, to_depth, step).wait_send()
            return carry

        lax.fori_loop(first, rows, body, 0)

    def halo_copies(tick):
        copies = []
        for side, target in ((0, left), (1, right)):
            there = 1 - side
            copies.append(
                pltpu.make_async_remote_copy(
                    src_ref=edge.at[tick, side], dst_ref=field_halo.at[tick, there],
                    send_sem=halo_send_sem.at[tick, 0, side], recv_sem=halo_recv_sem.at[tick, 0, there],
                    device_id=(depth, target), device_id_type=MESH,
                )
            )
        return copies

    def spec_copies(tick):
        copies = []
        for side, target in ((0, left), (1, right)):
            there = 1 - side
            copies.append(
                pltpu.make_async_remote_copy(
                    src_ref=spec_send.at[tick, side], dst_ref=spec_halo.at[tick, there],
                    send_sem=halo_send_sem.at[tick, 1, side], recv_sem=halo_recv_sem.at[tick, 1, there],
                    device_id=(depth, target), device_id_type=MESH,
                )
            )
        return copies

    def put_field(tick, part, a, value):
        term[0, part, a, 2 * HALO : 2 * HALO + slab] = value
        edge[tick, 0, part, a] = value[:HALO]
        edge[tick, 1, part, a] = value[slab - HALO :]

    def put_specimen(tick, a, values):
        for k in range(SLICES):
            coef[tick, k, a, HALO : HALO + slab] = contrast * values[k] - 4.0 * lat_slab
            damp[tick, k, a, HALO : HALO + slab] = contrast * values[SLICES + k]
        for kind in range(2):
            first, second = values[SLICES * kind], values[SLICES * kind + 1]
            top = jnp.concatenate([first[:HALO], second[:HALO]], axis=0)
            bottom = jnp.concatenate([first[slab - HALO :], second[slab - HALO :]], axis=0)
            spec_send[tick, 0, kind, a] = top.astype(jnp.bfloat16)
            spec_send[tick, 1, kind, a] = bottom.astype(jnp.bfloat16)

    def use_halos(tick):
        for copy in halo_copies(tick):
            copy.wait_recv()
        for copy in spec_copies(tick):
            copy.wait_recv()
        for side, start in ((0, 0), (1, HALO + slab)):
            off = (me == 0) if side == 0 else (me == rows - 1)
            keep = jnp.where(off, 0.0, 1.0)
            lat_here = lateral * keep
            for a in range(tiles):
                for part in range(2):
                    term[0, part, a, HALO + start : 2 * HALO + start] = field_halo[tick, side, part, a] * keep
                index = spec_halo[tick, side, 0, a].astype(jnp.float32)
                loss = spec_halo[tick, side, 1, a].astype(jnp.float32)
                for k in range(SLICES):
                    here = slice(k * HALO, (k + 1) * HALO)
                    coef[tick, k, a, start : start + HALO] = contrast * index[here] - 4.0 * lat_here
                    damp[tick, k, a, start : start + HALO] = contrast * loss[here]

    def one_term(tick, k, degree):
        src, dst = (degree - 1) % 2, degree % 2
        scale = 1.0 / degree
        lo, hi = HALO, HALO + tall
        centre, ahead_of, back_of = [], [], []
        for part in range(2):
            x = [term[src, part, a, lo:hi] for a in range(tiles)]
            centre.append(x)
            ahead_of.append([pltpu.roll(v, 1, 1) for v in x])
            back_of.append([pltpu.roll(v, LANES - 1, 1) for v in x])
        zero = jnp.zeros((tall, LANES), jnp.float32)
        for a in range(tiles):
            stirred = []
            for part in range(2):
                before = ahead_of[part][a - 1] if a > 0 else zero
                after = back_of[part][a + 1] if a < tiles - 1 else zero
                west = jnp.where(first_lane, before, ahead_of[part][a])
                east = jnp.where(last_lane, after, back_of[part][a])
                around = (term[src, part, a, lo - 1 : hi - 1] + term[src, part, a, lo + 1 : hi + 1]) + (west + east)
                stirred.append(lat * around + coef[tick, k, a] * centre[part][a])
            loss = damp[tick, k, a]
            new = [
                (-stirred[1] - loss * centre[0][a]) * scale,
                (stirred[0] - loss * centre[1][a]) * scale,
            ]
            for part in range(2):
                so_far = centre[part][a] if degree == 1 else total[part, a]
                if degree < TAYLOR:
                    term[dst, part, a, lo:hi] = new[part]
                    total[part, a] = so_far + new[part]
                else:
                    term[dst, part, a, lo:hi] = so_far + new[part]

    def march(tick):
        for k in range(SLICES):
            for degree in range(1, TAYLOR + 1):
                one_term(tick, k, degree)

    def convolve(load, store):
        for chunk in range(0, slab, 16):
            re = [load(0, a, chunk, 16) for a in range(tiles)]
            im = [load(1, a, chunk, 16) for a in range(tiles)]
            re, im = radix8(re, im, -1)
            for k1 in range(tiles):
                for part, value in ((0, re[k1]), (1, im[k1])):
                    at = slice(part * LANES, (part + 1) * LANES)
                    top = value.astype(jnp.bfloat16)
                    lhs[k1, chunk : chunk + 16, at] = top
                    lhs[k1, slab + chunk : slab + chunk + 16, at] = (value - top.astype(jnp.float32)).astype(jnp.bfloat16)
        for k1 in range(tiles):
            both = jnp.dot(lhs[k1], high_ref[k1], preferred_element_type=jnp.float32)
            rest = jnp.dot(lhs[k1, :slab], low_ref[k1], preferred_element_type=jnp.float32)
            mid[k1] = both[:slab] + (both[slab:] + rest)
        for chunk in range(0, slab, 16):
            re = [mid[k1, chunk : chunk + 16, :LANES] for k1 in range(tiles)]
            im = [mid[k1, chunk : chunk + 16, LANES:] for k1 in range(tiles)]
            re, im = radix8(re, im, 1)
            for a in range(tiles):
                store(0, a, chunk, 16, re[a])
                store(1, a, chunk, 16, im[a])

    def load_term(part, a, start, size):
        return term[0, part, a, 2 * HALO + start : 2 * HALO + start + size]

    def store_total(part, a, start, size, value):
        total[part, a, start : start + size] = value

    def load_total(part, a, start, size):
        return total[part, a, start : start + size]

    def pack(send):
        low64 = lane16 < 64
        for a in range(0, tiles, 2):
            stack = jnp.concatenate(
                [total[0, a, :slab], total[1, a, :slab], total[0, a + 1, :slab], total[1, a + 1, :slab]], axis=0
            )
            turned = stack.T
            for j in range(4):
                upper = turned[32 * j : 32 * j + 16]
                lower = turned[32 * j + 16 : 32 * j + 32]
                send[4 * a + j] = jnp.where(low64, upper, pltpu.roll(lower, 64, 1))
                send[4 * (a + 1) + j] = jnp.where(low64, pltpu.roll(upper, 64, 1), lower)

    def unpack(recv):
        for t in range(tiles):
            outs = swap_quarters([recv[4 * t + u] for u in range(4)], lane16)
            for c_high in range(2):
                for part in range(2):
                    total[part, t, 16 * c_high : 16 * c_high + 16] = outs[2 * c_high + part]

    for a in range(tiles):
        at = slice(a * LANES, (a + 1) * LANES)
        for part in range(2):
            put_field(0, part, a, field_ref[0, part, :, at])
        values = [ref[k, :, at].astype(jnp.float32) for ref in (index_ref, loss_ref) for k in range(SLICES)]
        put_specimen(0, a, values)
        turned = jnp.concatenate(values, axis=0).T
        for j in range(4):
            b_send[4 * a + j] = turned[32 * j : 32 * j + 32].astype(jnp.bfloat16)

    pl.semaphore_wait(barrier, 2 * rows - 1)
    for copy in halo_copies(0):
        copy.start()
    for copy in spec_copies(0):
        copy.start()
    start_all(b_send, b_recv, b_sems, depth, 1)
    b_recv[me] = b_send[me]

    use_halos(0)
    march(0)
    for load in loads:
        load.wait()
    convolve(load_term, store_total)
    pack(c_send)
    start_all(c_send, c_recv, c_sems, ahead, 0)

    wait_recv_all(b_send, b_recv, b_sems, depth, 1)
    for t in range(tiles):
        outs = swap_quarters([b_recv[4 * t + u].astype(jnp.float32) for u in range(4)], lane32)
        put_specimen(1, t, outs)
    for copy in spec_copies(1):
        copy.start()

    wait_recv_all(c_send, c_recv, c_sems, behind, 0)
    unpack(c_recv)

    def store_field(part, a, start, size, value):
        term[0, part, a, 2 * HALO + start : 2 * HALO + start + size] = value
        if start == 0:
            edge[1, 0, part, a] = value[:HALO]
        if start + size == slab:
            edge[1, 1, part, a] = value[size - HALO :]

    convolve(load_total, store_field)
    for copy in halo_copies(1):
        copy.start()
    use_halos(1)
    march(1)
    convolve(load_term, store_total)
    pack(d_send)
    start_all(d_send, d_recv, d_sems, depth, 1)
    d_recv[me] = d_send[me]
    wait_recv_all(d_send, d_recv, d_sems, depth, 1)
    unpack(d_recv)

    def store_out(part, a, start, size, value):
        out_ref[0, part, start : start + size, a * LANES : (a + 1) * LANES] = value

    convolve(load_total, store_out)

    for tick in range(2):
        for copy in halo_copies(tick) + spec_copies(tick):
            copy.wait_send()
    wait_send_all(b_send, b_recv, b_sems, depth, 1)
    wait_send_all(c_send, c_recv, c_sems, ahead, 0)
    wait_send_all(d_send, d_recv, d_sems, depth, 1)


def solution(mesh):
    groups, rows = mesh.shape["depth"], mesh.shape["rows"]

    def local(in_flight, phase_index, absorption):
        _, parts, slab, length = in_flight.shape
        tiles = length // LANES
        tall = slab + 2 * HALO
        high, low = middle_matrices(length)
        f32, bf16 = jnp.float32, jnp.bfloat16
        vmem = pl.BlockSpec(memory_space=pltpu.VMEM)
        return pl.pallas_call(
            functools.partial(kernel, groups, rows),
            out_shape=jax.ShapeDtypeStruct(in_flight.shape, f32),
            in_specs=[vmem, vmem, vmem, pl.BlockSpec(memory_space=pl.ANY), pl.BlockSpec(memory_space=pl.ANY)],
            out_specs=vmem,
            scratch_shapes=[
                pltpu.VMEM(high.shape, bf16),
                pltpu.VMEM(low.shape, bf16),
                pltpu.VMEM((2, parts, tiles, tall + 2 * HALO, LANES), f32),
                pltpu.VMEM((parts, tiles, tall, LANES), f32),
                pltpu.VMEM((2, SLICES, tiles, tall, LANES), f32),
                pltpu.VMEM((2, SLICES, tiles, tall, LANES), f32),
                pltpu.VMEM((2, 2, parts, tiles, HALO, LANES), f32),
                pltpu.VMEM((tiles, 2 * slab, 2 * LANES), bf16),
                pltpu.VMEM((tiles, slab, 2 * LANES), f32),
                pltpu.VMEM((2, 2, parts, tiles, HALO, LANES), f32),
                pltpu.VMEM((2, 2, 2, tiles, 2 * HALO, LANES), bf16),
                pltpu.VMEM((2, 2, 2, tiles, 2 * HALO, LANES), bf16),
                pltpu.VMEM((rows, 32, LANES), bf16),
                pltpu.VMEM((rows, 32, LANES), bf16),
                pltpu.VMEM((rows, 16, LANES), f32),
                pltpu.VMEM((rows, 16, LANES), f32),
                pltpu.VMEM((rows, 16, LANES), f32),
                pltpu.VMEM((rows, 16, LANES), f32),
                pltpu.SemaphoreType.DMA((2,)),
                pltpu.SemaphoreType.DMA((2, 2, 2)),
                pltpu.SemaphoreType.DMA((2, 2, 2)),
                pltpu.SemaphoreType.DMA((2, rows)),
                pltpu.SemaphoreType.DMA((2, rows)),
                pltpu.SemaphoreType.DMA((2, rows)),
            ],
            compiler_params=pltpu.CompilerParams(
                collective_id=0, has_side_effects=True, vmem_limit_bytes=32 * 1024 * 1024
            ),
        )(in_flight, phase_index, absorption, jnp.asarray(high), jnp.asarray(low))

    placed = (P("depth", None, "rows", None), P("depth", "rows", None), P("depth", "rows", None))
    return jax.shard_map(
        local, mesh=mesh, in_specs=placed, out_specs=P("depth", None, "rows", None), check_vma=False
    )
```

profile of v0, /device:TPU:6, one launch (start us, length us, event | category | flops | bytes accessed | tf_op | source)
XLA Modules:
  0.0 57.0 jit_solution(9467577585422317410)
XLA Ops:
  0.0 0.0 copy-start
  0.0 1.2 %copy-done = bf16[8,256,256]{2,1,0:T(8,128)(2,1)S(1)} copy-done((bf16[8,256,256]{2,1,0:T(8,128)(2,1)S(1)}, bf16[8,256,256]{2,1,0:T(8,128)(2,1)}, u32[]{:S(2)}) %copy-start) | copy-done | bytes 1048600
  1.2 0.0 copy-start.1
  1.2 1.2 %copy-done.1 = bf16[8,256,256]{2,1,0:T(8,128)(2,1)S(1)} copy-done((bf16[8,256,256]{2,1,0:T(8,128)(2,1)S(1)}, bf16[8,256,256]{2,1,0:T(8,128)(2,1)}, u32[]{:S(2)}) %copy-start.1) | copy-done | bytes 1048600
  2.5 0.0 copy-start.2
  2.5 0.9 %copy-done.2 = f32[1,2,32,1024]{3,2,1,0:T(8,128)S(1)} copy-done((f32[1,2,32,1024]{3,2,1,0:T(8,128)S(1)}, f32[1,2,32,1024]{3,2,1,0:T(8,128)}, u32[]{:S(2)}) %copy-start.2) | copy-done | bytes 262168
  3.4 0.0 copy-start.3
  3.4 0.9 %copy-done.3 = bf16[2,32,1024]{2,1,0:T(8,128)(2,1)S(1)} copy-done((bf16[2,32,1024]{2,1,0:T(8,128)(2,1)S(1)}, bf16[2,32,1024]{2,1,0:T(8,128)(2,1)}, u32[]{:S(2)}) %copy-start.3) | copy-done | bytes 131096
  4.3 0.0 copy-start.4
  4.3 0.9 %copy-done.4 = bf16[2,32,1024]{2,1,0:T(8,128)(2,1)S(1)} copy-done((bf16[2,32,1024]{2,1,0:T(8,128)(2,1)S(1)}, bf16[2,32,1024]{2,1,0:T(8,128)(2,1)}, u32[]{:S(2)}) %copy-start.4) | copy-done | bytes 131096
  5.2 51.0 %shard_map.55 = f32[1,2,32,1024]{3,2,1,0:T(8,128)S(1)} custom-call(f32[1,2,32,1024]{3,2,1,0:T(8,128)S(1)} %copy-done.2, bf16[2,32,1024]{2,1,0:T(8,128)(2,1)S(1)} %copy-done.3, bf16[2,32,1024]{2,1,0:T(8,128)(2,1)S(1)} %copy-done.4, bf16[8,256,256]{2,1,0:T(8,128)(2,1)S(1)} %copy-done.1, bf16[8,256,256]{2,1,0:T(8,128)(2,1)S(1)} %copy-done), custom_call_target="tpu_custom_call" | custom-call | tf_op jit(solution)/shard_map/pallas_call | solution.py:395
  56.2 0.7 %copy.7 = f32[1,2,32,1024]{3,2,1,0:T(8,128)} copy(f32[1,2,32,1024]{3,2,1,0:T(8,128)S(1)} %shard_map.55) | data formatting | bytes 524288
Async XLA Ops:
  0.0 1.2 %copy-start = (bf16[8,256,256]{2,1,0:T(8,128)(2,1)S(1)}, bf16[8,256,256]{2,1,0:T(8,128)(2,1)}, u32[]{:S(2)}) copy-start(bf16[8,256,256]{2,1,0:T(8,128)(2,1)} %constant.5.clone.low_hbm) | copy-start | bytes 3145732
  1.2 1.2 %copy-start.1 = (bf16[8,256,256]{2,1,0:T(8,128)(2,1)S(1)}, bf16[8,256,256]{2,1,0:T(8,128)(2,1)}, u32[]{:S(2)}) copy-start(bf16[8,256,256]{2,1,0:T(8,128)(2,1)} %constant.4.clone.high_hbm) | copy-start | bytes 3145732
  2.5 0.9 %copy-start.2 = (f32[1,2,32,1024]{3,2,1,0:T(8,128)S(1)}, f32[1,2,32,1024]{3,2,1,0:T(8,128)}, u32[]{:S(2)}) copy-start(f32[1,2,32,1024]{3,2,1,0:T(8,128)} %field_ref.1) | copy-start | bytes 786436
  3.4 0.9 %copy-start.3 = (bf16[2,32,1024]{2,1,0:T(8,128)(2,1)S(1)}, bf16[2,32,1024]{2,1,0:T(8,128)(2,1)}, u32[]{:S(2)}) copy-start(bf16[2,32,1024]{2,1,0:T(8,128)(2,1)} %index_ref.1) | copy-start | bytes 393220
  4.3 0.9 %copy-start.4 = (bf16[2,32,1024]{2,1,0:T(8,128)(2,1)S(1)}, bf16[2,32,1024]{2,1,0:T(8,128)(2,1)}, u32[]{:S(2)}) copy-start(bf16[2,32,1024]{2,1,0:T(8,128)(2,1)} %loss_ref.1) | copy-start | bytes 393220
where the time goes:
time: 57.2 us; the launch traced here: 57 us
  Pallas kernels  51 us (89%)
  local copies, waits for them, and re-layouts  5.91 us (10%)
    pallas_call x1, Pallas kernels, local(): pl.pallas_call(functools.partial(kernel, groups, rows), out_shape=jax.Sha...  51 us
    unnamed x11, local copies, waits for them, and re-layouts  5.91 us

commit v1 on v0

v1 whole, which is shorter than its diff:
```python
import functools
import math

import jax
import jax.numpy as jnp
import ml_dtypes
import numpy as np
from jax import lax
from jax.experimental import pallas as pl
from jax.experimental.pallas import tpu as pltpu
from jax.sharding import PartitionSpec as P

TAYLOR = 4
SLICES = 2
HALO = 8
CHUNK = 16
PLANE_WIDTH = 4
LANES = 128
lateral = 0.22
contrast = 0.2
MESH = pl.DeviceIdType.MESH


def middle_matrices(length):
    coarse = length // LANES
    b = np.arange(LANES)
    k = np.arange(length)
    f = np.where(k < length // 2, k, k - length)
    gain = np.exp(-1j * np.pi * ((f * f) % (8 * length)) / (4 * length))
    dft = np.exp(-2j * np.pi * (np.outer(b, b) % LANES) / LANES)
    whole = np.zeros((coarse, 2 * LANES, 2 * LANES))
    for k1 in range(coarse):
        twiddle = np.exp(-2j * np.pi * b * k1 / length)
        m = (twiddle[:, None] * dft * gain[k1 + coarse * b][None, :]) @ (np.conj(dft) * np.conj(twiddle)[None, :])
        m = m / length
        whole[k1] = np.block([[m.real, m.imag], [-m.imag, m.real]])
    high = whole.astype(np.float32).astype(ml_dtypes.bfloat16)
    low = (whole - high.astype(np.float64)).astype(np.float32).astype(ml_dtypes.bfloat16)
    return high, low


def radix8(re, im, sign):
    half = math.sqrt(0.5)

    def turn(r, i):
        return (-i, r) if sign > 0 else (i, -r)

    def four(r, i):
        a, b = (r[0] + r[2], i[0] + i[2]), (r[0] - r[2], i[0] - i[2])
        c, d = (r[1] + r[3], i[1] + i[3]), (r[1] - r[3], i[1] - i[3])
        d = turn(*d)
        return [(a[0] + c[0], a[1] + c[1]), (b[0] + d[0], b[1] + d[1]), (a[0] - c[0], a[1] - c[1]), (b[0] - d[0], b[1] - d[1])]

    even = four(re[0::2], im[0::2])
    odd = four(re[1::2], im[1::2])
    s = 1.0 if sign > 0 else -1.0
    o1, o3 = odd[1], odd[3]
    odd[1] = ((o1[0] - s * o1[1]) * half, (o1[1] + s * o1[0]) * half)
    odd[2] = turn(*odd[2])
    odd[3] = ((-o3[0] - s * o3[1]) * half, (-o3[1] + s * o3[0]) * half)
    out = [(e[0] + o[0], e[1] + o[1]) for e, o in zip(even, odd)]
    out += [(e[0] - o[0], e[1] - o[1]) for e, o in zip(even, odd)]
    return [v[0] for v in out], [v[1] for v in out]


def far_first(height, width):
    def centred(v, n):
        return v if v <= n // 2 else v - n

    left = [(centred(y, height), centred(x, width)) for y in range(height) for x in range(width) if y or x]
    left.sort(key=lambda t: -(abs(t[0]) + abs(t[1])))
    order = []
    while left:
        t = left.pop(0)
        order.append(t)
        opposite = [u for u in left if (u[0] + t[0]) % height == 0 and (u[1] + t[1]) % width == 0]
        if opposite:
            left.remove(opposite[0])
            order.append(opposite[0])
    return order


def swap_quarters(vs, lane):
    low64 = lane < 64
    low32 = lax.rem(lane, 64) < 32

    def roll(x, by):
        return pltpu.roll(x, by, 1)

    a0 = jnp.where(low64, vs[0], roll(vs[2], 64))
    a2 = jnp.where(low64, roll(vs[0], 64), vs[2])
    a1 = jnp.where(low64, vs[1], roll(vs[3], 64))
    a3 = jnp.where(low64, roll(vs[1], 64), vs[3])
    return [
        jnp.where(low32, a0, roll(a1, 32)),
        jnp.where(low32, roll(a0, 96), a1),
        jnp.where(low32, a2, roll(a3, 32)),
        jnp.where(low32, roll(a2, 96), a3),
    ]


def kernel(
    groups, rows, width, field_hbm, index_hbm, loss_hbm, high_hbm, low_hbm, out_ref,
    field_ref, index_ref, loss_ref, high_ref, low_ref, term, total, coef, damp, edge, lhs, mid,
    first_field_halo, first_spec_halo, field_halo, spec_send, spec_halo,
    b_send, b_recv, c_send, c_recv, d_send, d_recv,
    load_sem, first_sems, halo_sems, b_sems, c_sems, d_sems,
):
    depth = lax.axis_index("depth")
    me = lax.axis_index("rows")
    ahead = lax.rem(depth + 1, groups)
    behind = lax.rem(depth + groups - 1, groups)
    right, left = lax.rem(me + 1, rows), lax.rem(me + rows - 1, rows)
    tiles = high_ref.shape[0]
    slab = field_ref.shape[2]
    tall = slab + 2 * HALO

    barrier = pltpu.get_barrier_semaphore()

    def greet(step, carry):
        pl.semaphore_signal(barrier, inc=1, device_id=(depth, lax.rem(me + step, rows)), device_id_type=MESH)
        return carry

    def greet_behind(step, carry):
        pl.semaphore_signal(barrier, inc=1, device_id=(behind, lax.rem(me + step, rows)), device_id_type=MESH)
        return carry

    lax.fori_loop(1, rows, greet, 0)
    lax.fori_loop(0, rows, greet_behind, 0)

    pairs = ((field_hbm, field_ref), (index_hbm, index_ref), (loss_hbm, loss_ref), (high_hbm, high_ref), (low_hbm, low_ref))
    loads = [pltpu.make_async_copy(src, dst, load_sem.at[i]) for i, (src, dst) in enumerate(pairs)]
    for load in loads:
        load.start()

    lane32 = lax.broadcasted_iota(jnp.int32, (32, LANES), 1)
    lane16 = lax.broadcasted_iota(jnp.int32, (16, LANES), 1)
    row_tall = lax.broadcasted_iota(jnp.int32, (tall, LANES), 0)
    outside = ((row_tall < HALO) & (me == 0)) | ((row_tall >= HALO + slab) & (me == rows - 1))
    lat = jnp.where(outside, 0.0, lateral)
    lat_slab = jnp.full((slab, LANES), lateral, jnp.float32)

    for slot in range(2):
        for part in range(2):
            for a in range(tiles):
                term[slot, part, a, 0:HALO] = jnp.zeros((HALO, LANES), jnp.float32)
                term[slot, part, a, tall + HALO : tall + 2 * HALO] = jnp.zeros((HALO, LANES), jnp.float32)

    own_y, own_x = me // width, lax.rem(me, width)
    height = rows // width
    order = far_first(height, width)

    def start_all(src, dst, sems, to_depth, with_self):
        for dy, dx in order + ([(0, 0)] if with_self else []):
            target = lax.rem(own_y + (dy + height), height) * width + lax.rem(own_x + (dx + width), width)
            pltpu.make_async_remote_copy(
                src_ref=src.at[target], dst_ref=dst.at[me], send_sem=sems.at[0], recv_sem=sems.at[1],
                device_id=(to_depth, target), device_id_type=MESH,
            ).start()

    def whole(src, dst, sems, with_self):
        count = rows if with_self else rows - 1
        return pltpu.make_async_remote_copy(
            src_ref=src.at[pl.ds(0, count)], dst_ref=dst.at[pl.ds(0, count)], send_sem=sems.at[0], recv_sem=sems.at[1],
            device_id=(depth, right), device_id_type=MESH,
        )

    def first_halo_copies():
        copies = []
        for side, target in ((0, left), (1, right)):
            there = 1 - side
            here = pl.ds(0 if side == 0 else slab - HALO, HALO)
            triples = (
                (field_hbm.at[0, :, here, :], first_field_halo.at[there]),
                (index_hbm.at[:, here, :], first_spec_halo.at[there, 0]),
                (loss_hbm.at[:, here, :], first_spec_halo.at[there, 1]),
            )
            for n, (src, dst) in enumerate(triples):
                copies.append(
                    pltpu.make_async_remote_copy(
                        src_ref=src, dst_ref=dst,
                        send_sem=first_sems.at[0, n, side], recv_sem=first_sems.at[1, n, there],
                        device_id=(depth, target), device_id_type=MESH,
                    )
                )
        return copies

    def halo_copies(src, dst, kind):
        copies = []
        for side, target in ((0, left), (1, right)):
            there = 1 - side
            copies.append(
                pltpu.make_async_remote_copy(
                    src_ref=src.at[side], dst_ref=dst.at[there],
                    send_sem=halo_sems.at[0, kind, side], recv_sem=halo_sems.at[1, kind, there],
                    device_id=(depth, target), device_id_type=MESH,
                )
            )
        return copies

    def put_coefficients(tick, a, values):
        for k in range(SLICES):
            coef[tick, k, a, HALO : HALO + slab] = contrast * values[k] - 4.0 * lat_slab
            damp[tick, k, a, HALO : HALO + slab] = contrast * values[SLICES + k]

    def put_spec_edges(a, values):
        for kind in range(2):
            first, second = values[SLICES * kind], values[SLICES * kind + 1]
            top = jnp.concatenate([first[:HALO], second[:HALO]], axis=0)
            bottom = jnp.concatenate([first[slab - HALO :], second[slab - HALO :]], axis=0)
            spec_send[0, kind, a] = top.astype(jnp.bfloat16)
            spec_send[1, kind, a] = bottom.astype(jnp.bfloat16)

    def use_halos(tick, field_of, spec_of):
        for side, start in ((0, 0), (1, HALO + slab)):
            off = (me == 0) if side == 0 else (me == rows - 1)
            keep = jnp.where(off, 0.0, 1.0)
            lat_here = lateral * keep
            for a in range(tiles):
                for part in range(2):
                    term[0, part, a, HALO + start : 2 * HALO + start] = field_of(side, part, a) * keep
                for k in range(SLICES):
                    coef[tick, k, a, start : start + HALO] = contrast * spec_of(side, 0, k, a) - 4.0 * lat_here
                    damp[tick, k, a, start : start + HALO] = contrast * spec_of(side, 1, k, a)

    lane_chunk = lax.broadcasted_iota(jnp.int32, (CHUNK, LANES), 1)
    first_lane = lane_chunk == 0
    last_lane = lane_chunk == LANES - 1
    nothing = jnp.zeros((CHUNK, LANES), jnp.float32)

    def one_term(tick, k, degree):
        src, dst = (degree - 1) % 2, degree % 2
        scale = 1.0 / degree
        final = k == SLICES - 1 and degree == TAYLOR
        for r in range(HALO if final else 0, HALO + slab if final else tall, CHUNK):
            at = slice(r, r + CHUNK)
            lo, hi = HALO + r, HALO + r + CHUNK

            def fetch(a):
                if a < 0 or a >= tiles:
                    return [(nothing, nothing, nothing)] * 2
                xs = [term[src, part, a, lo:hi] for part in range(2)]
                return [(x, pltpu.roll(x, 1, 1), pltpu.roll(x, LANES - 1, 1)) for x in xs]

            before, here = fetch(-1), fetch(0)
            for a in range(tiles):
                after = fetch(a + 1)
                stirred = []
                for part in range(2):
                    west = jnp.where(first_lane, before[part][1], here[part][1])
                    east = jnp.where(last_lane, after[part][2], here[part][2])
                    beside = term[src, part, a, lo - 1 : hi - 1] + term[src, part, a, lo + 1 : hi + 1]
                    stirred.append(lat[at] * (beside + (west + east)) + coef[tick, k, a, at] * here[part][0])
                loss = damp[tick, k, a, at]
                new = [
                    (stirred[1] + loss * here[0][0]) * (-scale),
                    (stirred[0] - loss * here[1][0]) * scale,
                ]
                for part in range(2):
                    so_far = here[part][0] if degree == 1 else total[part, a, at]
                    if degree < TAYLOR:
                        term[dst, part, a, lo:hi] = new[part]
                        total[part, a, at] = so_far + new[part]
                    else:
                        term[dst, part, a, lo:hi] = so_far + new[part]
                before, here = here, after

    def march(tick):
        for k in range(SLICES):
            for degree in range(1, TAYLOR + 1):
                one_term(tick, k, degree)

    def convolve(load, store):
        for chunk in range(0, slab, 16):
            re = [load(0, a, chunk, 16) for a in range(tiles)]
            im = [load(1, a, chunk, 16) for a in range(tiles)]
            re, im = radix8(re, im, -1)
            for k1 in range(tiles):
                for part, value in ((0, re[k1]), (1, im[k1])):
                    at = slice(part * LANES, (part + 1) * LANES)
                    top = value.astype(jnp.bfloat16)
                    lhs[k1, chunk : chunk + 16, at] = top
                    lhs[k1, slab + chunk : slab + chunk + 16, at] = (value - top.astype(jnp.float32)).astype(jnp.bfloat16)
        for k1 in range(tiles):
            both = jnp.dot(lhs[k1], high_ref[k1], preferred_element_type=jnp.float32)
            rest = jnp.dot(lhs[k1, :slab], low_ref[k1], preferred_element_type=jnp.float32)
            mid[k1] = both[:slab] + (both[slab:] + rest)
        for chunk in range(0, slab, 16):
            re = [mid[k1, chunk : chunk + 16, :LANES] for k1 in range(tiles)]
            im = [mid[k1, chunk : chunk + 16, LANES:] for k1 in range(tiles)]
            re, im = radix8(re, im, 1)
            for a in range(tiles):
                store(0, a, chunk, 16, re[a])
                store(1, a, chunk, 16, im[a])

    def load_term(part, a, start, size):
        return term[0, part, a, 2 * HALO + start : 2 * HALO + start + size]

    def store_total(part, a, start, size, value):
        total[part, a, start : start + size] = value

    def load_total(part, a, start, size):
        return total[part, a, start : start + size]

    def pack(send):
        low64 = lane16 < 64
        for a in range(0, tiles, 2):
            stack = jnp.concatenate(
                [total[0, a, :slab], total[1, a, :slab], total[0, a + 1, :slab], total[1, a + 1, :slab]], axis=0
            )
            turned = stack.T
            for j in range(4):
                upper = turned[32 * j : 32 * j + 16]
                lower = turned[32 * j + 16 : 32 * j + 32]
                send[4 * a + j] = jnp.where(low64, upper, pltpu.roll(lower, 64, 1))
                send[4 * (a + 1) + j] = jnp.where(low64, pltpu.roll(upper, 64, 1), lower)

    def unpack(recv):
        for t in range(tiles):
            outs = swap_quarters([recv[4 * t + u] for u in range(4)], lane16)
            for c_high in range(2):
                for part in range(2):
                    total[part, t, 16 * c_high : 16 * c_high + 16] = outs[2 * c_high + part]

    pl.semaphore_wait(barrier, 2 * rows - 1)
    for copy in first_halo_copies():
        copy.start()

    for load in loads[:3]:
        load.wait()
    for a in range(tiles):
        at = slice(a * LANES, (a + 1) * LANES)
        for part in range(2):
            term[0, part, a, 2 * HALO : 2 * HALO + slab] = field_ref[0, part, :, at]
        values = [ref[k, :, at].astype(jnp.float32) for ref in (index_ref, loss_ref) for k in range(SLICES)]
        put_coefficients(0, a, values)
        turned = jnp.concatenate(values, axis=0).T
        for j in range(4):
            b_send[4 * a + j] = turned[32 * j : 32 * j + 32].astype(jnp.bfloat16)
    start_all(b_send, b_recv, b_sems, depth, False)
    b_recv[me] = b_send[me]

    for copy in first_halo_copies():
        copy.wait_recv()
    use_halos(
        0,
        lambda side, part, a: first_field_halo[side, part, :, a * LANES : (a + 1) * LANES],
        lambda side, kind, k, a: first_spec_halo[side, kind, k, :, a * LANES : (a + 1) * LANES].astype(jnp.float32),
    )
    march(0)
    for load in loads[3:]:
        load.wait()
    convolve(load_term, store_total)
    pack(c_send)
    start_all(c_send, c_recv, c_sems, ahead, True)

    whole(b_send, b_recv, b_sems, False).wait_recv()
    for t in range(tiles):
        outs = swap_quarters([b_recv[4 * t + u].astype(jnp.float32) for u in range(4)], lane32)
        put_coefficients(1, t, outs)
        put_spec_edges(t, outs)
    spec_copies = halo_copies(spec_send, spec_halo, 1)
    for copy in spec_copies:
        copy.start()

    whole(c_send, c_recv, c_sems, True).wait_recv()
    unpack(c_recv)

    def store_field(part, a, start, size, value):
        term[0, part, a, 2 * HALO + start : 2 * HALO + start + size] = value
        if start == 0:
            edge[0, part, a] = value[:HALO]
        if start + size == slab:
            edge[1, part, a] = value[size - HALO :]

    convolve(load_total, store_field)
    field_copies = halo_copies(edge, field_halo, 0)
    for copy in field_copies:
        copy.start()
    for copy in field_copies + spec_copies:
        copy.wait_recv()
    use_halos(
        1,
        lambda side, part, a: field_halo[side, part, a],
        lambda side, kind, k, a: spec_halo[side, kind, a].astype(jnp.float32)[k * HALO : (k + 1) * HALO],
    )
    march(1)
    convolve(load_term, store_total)
    pack(d_send)
    start_all(d_send, d_recv, d_sems, depth, False)
    d_recv[me] = d_send[me]
    whole(d_send, d_recv, d_sems, False).wait_recv()
    unpack(d_recv)

    def store_out(part, a, start, size, value):
        out_ref[0, part, start : start + size, a * LANES : (a + 1) * LANES] = value

    convolve(load_total, store_out)

    for copy in first_halo_copies() + spec_copies + field_copies:
        copy.wait_send()
    whole(b_send, b_recv, b_sems, False).wait_send()
    whole(c_send, c_recv, c_sems, True).wait_send()
    whole(d_send, d_recv, d_sems, False).wait_send()


def solution(mesh):
    groups, rows = mesh.shape["depth"], mesh.shape["rows"]

    def local(in_flight, phase_index, absorption):
        _, parts, slab, length = in_flight.shape
        tiles = length // LANES
        tall = slab + 2 * HALO
        high, low = middle_matrices(length)
        f32, bf16 = jnp.float32, jnp.bfloat16
        vmem = pl.BlockSpec(memory_space=pltpu.VMEM)
        return pl.pallas_call(
            functools.partial(kernel, groups, rows, PLANE_WIDTH),
            out_shape=jax.ShapeDtypeStruct(in_flight.shape, f32),
            in_specs=[pl.BlockSpec(memory_space=pltpu.HBM)] * 5,
            out_specs=vmem,
            scratch_shapes=[
                pltpu.VMEM(in_flight.shape, f32),
                pltpu.VMEM(phase_index.shape, bf16),
                pltpu.VMEM(absorption.shape, bf16),
                pltpu.VMEM(high.shape, bf16),
                pltpu.VMEM(low.shape, bf16),
                pltpu.VMEM((2, parts, tiles, tall + 2 * HALO, LANES), f32),
                pltpu.VMEM((parts, tiles, tall, LANES), f32),
                pltpu.VMEM((2, SLICES, tiles, tall, LANES), f32),
                pltpu.VMEM((2, SLICES, tiles, tall, LANES), f32),
                pltpu.VMEM((2, parts, tiles, HALO, LANES), f32),
                pltpu.VMEM((tiles, 2 * slab, 2 * LANES), bf16),
                pltpu.VMEM((tiles, slab, 2 * LANES), f32),
                pltpu.VMEM((2, parts, HALO, length), f32),
                pltpu.VMEM((2, 2, SLICES, HALO, length), bf16),
                pltpu.VMEM((2, parts, tiles, HALO, LANES), f32),
                pltpu.VMEM((2, 2, tiles, 2 * HALO, LANES), bf16),
                pltpu.VMEM((2, 2, tiles, 2 * HALO, LANES), bf16),
                pltpu.VMEM((rows, 32, LANES), bf16),
                pltpu.VMEM((rows, 32, LANES), bf16),
                pltpu.VMEM((rows, 16, LANES), f32),
                pltpu.VMEM((rows, 16, LANES), f32),
                pltpu.VMEM((rows, 16, LANES), f32),
                pltpu.VMEM((rows, 16, LANES), f32),
                pltpu.SemaphoreType.DMA((5,)),
                pltpu.SemaphoreType.DMA((2, 3, 2)),
                pltpu.SemaphoreType.DMA((2, 2, 2)),
                pltpu.SemaphoreType.DMA((2,)),
                pltpu.SemaphoreType.DMA((2,)),
                pltpu.SemaphoreType.DMA((2,)),
            ],
            compiler_params=pltpu.CompilerParams(
                collective_id=0, has_side_effects=True, vmem_limit_bytes=60 * 1024 * 1024
            ),
        )(in_flight, phase_index, absorption, jnp.asarray(high), jnp.asarray(low))

    placed = (P("depth", None, "rows", None), P("depth", "rows", None), P("depth", "rows", None))
    return jax.shard_map(
        local, mesh=mesh, in_specs=placed, out_specs=P("depth", None, "rows", None), check_vma=False
    )
```

time: 57.2 us -> 48.5 us (0.85)
  Pallas kernels: 51 us -> 46.6 us
  local copies, waits for them, and re-layouts: 5.91 us -> 1.67 us
    pallas_call x1, Pallas kernels: 51 us -> 46.6 us  [local(): pl.pallas_call(functools.partial(kernel, groups, rows, PLANE_WIDTH), out_...]
    unnamed x11 -> x1, local copies, waits for them, and re-layouts: 5.91 us -> 1.67 us
where the time goes in v1:
time: 48.5 us; the launch traced here: 48.3 us
  Pallas kernels  46.6 us (96%)
  local copies, waits for them, and re-layouts  1.67 us (3%)
    pallas_call x1, Pallas kernels, local(): pl.pallas_call(functools.partial(kernel, groups, rows, PLANE_WIDTH), out_...  46.6 us
    unnamed x1, local copies, waits for them, and re-layouts  1.67 us

profile of v1, /device:TPU:6, one launch (start us, length us, event | category | flops | bytes accessed | tf_op | source)
XLA Modules:
  0.0 48.3 jit_solution(447234526210490211)
XLA Ops:
  0.0 46.6 %shard_map.55 = f32[1,2,32,1024]{3,2,1,0:T(8,128)} custom-call(f32[1,2,32,1024]{3,2,1,0:T(8,128)} %field_hbm.1, bf16[2,32,1024]{2,1,0:T(8,128)(2,1)} %index_hbm.1, bf16[2,32,1024]{2,1,0:T(8,128)(2,1)} %loss_hbm.1, bf16[8,256,256]{2,1,0:T(8,128)(2,1)} %constant.4.clone.high_hbm, bf16[8,256,256]{2,1,0:T(8,128)(2,1)} %constant.5.clone.low_hbm), custom_call_target="tpu_custom_call" | custom-call | tf_op jit(solution)/shard_map/pallas_call | solution.py:417
  46.6 1.7 %copy.7 = f32[1,2,32,1024]{3,2,1,0:T(8,128)} copy(f32[1,2,32,1024]{3,2,1,0:T(8,128)} %shard_map.55) | data formatting | bytes 524288

commit v2 on v1

--- a/solution.py
+++ b/solution.py
@@ -101,8 +101,8 @@
 
 def kernel(
     groups, rows, width, field_hbm, index_hbm, loss_hbm, high_hbm, low_hbm, out_ref,
-    field_ref, index_ref, loss_ref, high_ref, low_ref, term, total, coef, damp, edge, lhs, mid,
-    first_field_halo, first_spec_halo, field_halo, spec_send, spec_halo,
+    field_ref, index_ref, loss_ref, high_ref, low_ref, term, total, coef, damp, lhs, mid,
+    first_field_halo, first_spec_halo, spec_send, spec_halo,
     b_send, b_recv, c_send, c_recv, d_send, d_recv,
     load_sem, first_sems, halo_sems, b_sems, c_sems, d_sems,
 ):
@@ -126,14 +126,14 @@
         return carry
 
     lax.fori_loop(1, rows, greet, 0)
-    lax.fori_loop(0, rows, greet_behind, 0)
-
     pairs = ((field_hbm, field_ref), (index_hbm, index_ref), (loss_hbm, loss_ref), (high_hbm, high_ref), (low_hbm, low_ref))
     loads = [pltpu.make_async_copy(src, dst, load_sem.at[i]) for i, (src, dst) in enumerate(pairs)]
     for load in loads:
         load.start()
+    lax.fori_loop(0, rows, greet_behind, 0)
 
     lane32 = lax.broadcasted_iota(jnp.int32, (32, LANES), 1)
+    lane8 = lax.broadcasted_iota(jnp.int32, (8, LANES), 1)
     lane16 = lax.broadcasted_iota(jnp.int32, (16, LANES), 1)
     row_tall = lax.broadcasted_iota(jnp.int32, (tall, LANES), 0)
     outside = ((row_tall < HALO) & (me == 0)) | ((row_tall >= HALO + slab) & (me == rows - 1))
@@ -217,7 +217,7 @@
             keep = jnp.where(off, 0.0, 1.0)
             lat_here = lateral * keep
             for a in range(tiles):
-                for part in range(2):
+                for part in range(2) if field_of else ():
                     term[0, part, a, HALO + start : 2 * HALO + start] = field_of(side, part, a) * keep
                 for k in range(SLICES):
                     coef[tick, k, a, start : start + HALO] = contrast * spec_of(side, 0, k, a) - 4.0 * lat_here
@@ -270,7 +270,7 @@
             for degree in range(1, TAYLOR + 1):
                 one_term(tick, k, degree)
 
-    def convolve(load, store):
+    def convolve(load, store, slab=slab):
         for chunk in range(0, slab, 16):
             re = [load(0, a, chunk, 16) for a in range(tiles)]
             im = [load(1, a, chunk, 16) for a in range(tiles)]
@@ -282,9 +282,9 @@
                     lhs[k1, chunk : chunk + 16, at] = top
                     lhs[k1, slab + chunk : slab + chunk + 16, at] = (value - top.astype(jnp.float32)).astype(jnp.bfloat16)
         for k1 in range(tiles):
-            both = jnp.dot(lhs[k1], high_ref[k1], preferred_element_type=jnp.float32)
+            both = jnp.dot(lhs[k1, : 2 * slab], high_ref[k1], preferred_element_type=jnp.float32)
             rest = jnp.dot(lhs[k1, :slab], low_ref[k1], preferred_element_type=jnp.float32)
-            mid[k1] = both[:slab] + (both[slab:] + rest)
+            mid[k1, :slab] = both[:slab] + (both[slab:] + rest)
         for chunk in range(0, slab, 16):
             re = [mid[k1, chunk : chunk + 16, :LANES] for k1 in range(tiles)]
             im = [mid[k1, chunk : chunk + 16, LANES:] for k1 in range(tiles)]
@@ -312,33 +312,57 @@
             for j in range(4):
                 upper = turned[32 * j : 32 * j + 16]
                 lower = turned[32 * j + 16 : 32 * j + 32]
-                send[4 * a + j] = jnp.where(low64, upper, pltpu.roll(lower, 64, 1))
-                send[4 * (a + 1) + j] = jnp.where(low64, pltpu.roll(upper, 64, 1), lower)
-
-    def unpack(recv):
+                send[4 * a + j, 0:16] = jnp.where(low64, upper, pltpu.roll(lower, 64, 1))
+                send[4 * (a + 1) + j, 0:16] = jnp.where(low64, pltpu.roll(upper, 64, 1), lower)
+
+    def unpack(recv, first):
         for t in range(tiles):
-            outs = swap_quarters([recv[4 * t + u] for u in range(4)], lane16)
+            outs = swap_quarters([recv[4 * t + u, 0:16] for u in range(4)], lane16)
             for c_high in range(2):
                 for part in range(2):
-                    total[part, t, 16 * c_high : 16 * c_high + 16] = outs[2 * c_high + part]
-
-    pl.semaphore_wait(barrier, 2 * rows - 1)
-    for copy in first_halo_copies():
-        copy.start()
-
-    for load in loads[:3]:
+                    at = first + 16 * c_high
+                    total[part, t, at : at + 16] = outs[2 * c_high + part]
+
+    def pack_halos(send):
+        low = lane8 < 64
+        for r in range(rows):
+            joined = jnp.where(low, send[(r + 1) % rows, 0:8], send[(r + rows - 1) % rows, 8:16])
+            send[r, 16:24] = pltpu.roll(joined, 64, 1)
+
+    def unpack_halos(recv):
+        keeps = [jnp.where(me == edge_at, 0.0, 1.0) for edge_at in (0, rows - 1)]
+        for t in range(tiles):
+            outs = swap_quarters([recv[4 * t + u, 16:24] for u in range(4)], lane8)
+            for side, start in ((0, 0), (1, HALO + slab)):
+                for part in range(2):
+                    total[part, t, start : start + HALO] = outs[2 * side + part] * keeps[side]
+
+    def specimen(a):
+        at = slice(a * LANES, (a + 1) * LANES)
+        return [ref[k, :, at].astype(jnp.float32) for ref in (index_ref, loss_ref) for k in range(SLICES)]
+
+    def pack_specimen():
+        for a in range(tiles):
+            turned = jnp.concatenate(specimen(a), axis=0).T
+            for j in range(4):
+                b_send[4 * a + j] = turned[32 * j : 32 * j + 32].astype(jnp.bfloat16)
+        b_recv[me] = b_send[me]
+
+    def enter():
+        pl.semaphore_wait(barrier, 2 * rows - 1)
+        for copy in first_halo_copies():
+            copy.start()
+
+    for load in loads[1:3]:
         load.wait()
+    pack_specimen()
+    enter()
+    start_all(b_send, b_recv, b_sems, depth, False)
+    loads[0].wait()
     for a in range(tiles):
-        at = slice(a * LANES, (a + 1) * LANES)
         for part in range(2):
-            term[0, part, a, 2 * HALO : 2 * HALO + slab] = field_ref[0, part, :, at]
-        values = [ref[k, :, at].astype(jnp.float32) for ref in (index_ref, loss_ref) for k in range(SLICES)]
-        put_coefficients(0, a, values)
-        turned = jnp.concatenate(values, axis=0).T
-        for j in range(4):
-            b_send[4 * a + j] = turned[32 * j : 32 * j + 32].astype(jnp.bfloat16)
-    start_all(b_send, b_recv, b_sems, depth, False)
-    b_recv[me] = b_send[me]
+            term[0, part, a, 2 * HALO : 2 * HALO + slab] = field_ref[0, part, :, a * LANES : (a + 1) * LANES]
+        put_coefficients(0, a, specimen(a))
 
     for copy in first_halo_copies():
         copy.wait_recv()
@@ -352,6 +376,7 @@
         load.wait()
     convolve(load_term, store_total)
     pack(c_send)
+    pack_halos(c_send)
     start_all(c_send, c_recv, c_sems, ahead, True)
 
     whole(b_send, b_recv, b_sems, False).wait_recv()
@@ -364,24 +389,18 @@
         copy.start()
 
     whole(c_send, c_recv, c_sems, True).wait_recv()
-    unpack(c_recv)
+    unpack(c_recv, HALO)
+    unpack_halos(c_recv)
 
     def store_field(part, a, start, size, value):
-        term[0, part, a, 2 * HALO + start : 2 * HALO + start + size] = value
-        if start == 0:
-            edge[0, part, a] = value[:HALO]
-        if start + size == slab:
-            edge[1, part, a] = value[size - HALO :]
-
-    convolve(load_total, store_field)
-    field_copies = halo_copies(edge, field_halo, 0)
-    for copy in field_copies:
-        copy.start()
-    for copy in field_copies + spec_copies:
+        term[0, part, a, HALO + start : HALO + start + size] = value
+
+    convolve(load_total, store_field, tall)
+    for copy in spec_copies:
         copy.wait_recv()
     use_halos(
         1,
-        lambda side, part, a: field_halo[side, part, a],
+        None,
         lambda side, kind, k, a: spec_halo[side, kind, a].astype(jnp.float32)[k * HALO : (k + 1) * HALO],
     )
     march(1)
@@ -390,14 +409,14 @@
     start_all(d_send, d_recv, d_sems, depth, False)
     d_recv[me] = d_send[me]
     whole(d_send, d_recv, d_sems, False).wait_recv()
-    unpack(d_recv)
+    unpack(d_recv, 0)
 
     def store_out(part, a, start, size, value):
         out_ref[0, part, start : start + size, a * LANES : (a + 1) * LANES] = value
 
     convolve(load_total, store_out)
 
-    for copy in first_halo_copies() + spec_copies + field_copies:
+    for copy in first_halo_copies() + spec_copies:
         copy.wait_send()
     whole(b_send, b_recv, b_sems, False).wait_send()
     whole(c_send, c_recv, c_sems, True).wait_send()
@@ -429,18 +448,16 @@
                 pltpu.VMEM((parts, tiles, tall, LANES), f32),
                 pltpu.VMEM((2, SLICES, tiles, tall, LANES), f32),
                 pltpu.VMEM((2, SLICES, tiles, tall, LANES), f32),
-                pltpu.VMEM((2, parts, tiles, HALO, LANES), f32),
-                pltpu.VMEM((tiles, 2 * slab, 2 * LANES), bf16),
-                pltpu.VMEM((tiles, slab, 2 * LANES), f32),
+                pltpu.VMEM((tiles, 2 * tall, 2 * LANES), bf16),
+                pltpu.VMEM((tiles, tall, 2 * LANES), f32),
                 pltpu.VMEM((2, parts, HALO, length), f32),
                 pltpu.VMEM((2, 2, SLICES, HALO, length), bf16),
-                pltpu.VMEM((2, parts, tiles, HALO, LANES), f32),
                 pltpu.VMEM((2, 2, tiles, 2 * HALO, LANES), bf16),
                 pltpu.VMEM((2, 2, tiles, 2 * HALO, LANES), bf16),
                 pltpu.VMEM((rows, 32, LANES), bf16),
                 pltpu.VMEM((rows, 32, LANES), bf16),
-                pltpu.VMEM((rows, 16, LANES), f32),
-                pltpu.VMEM((rows, 16, LANES), f32),
+                pltpu.VMEM((rows, 24, LANES), f32),
+                pltpu.VMEM((rows, 24, LANES), f32),
                 pltpu.VMEM((rows, 16, LANES), f32),
                 pltpu.VMEM((rows, 16, LANES), f32),
                 pltpu.SemaphoreType.DMA((5,)),
@@ -451,9 +468,9 @@
                 pltpu.SemaphoreType.DMA((2,)),
             ],
             compiler_params=pltpu.CompilerParams(
-                collective_id=0, has_side_effects=True, vmem_limit_bytes=60 * 1024 * 1024
+                collective_id=0, has_side_effects=True, vmem_limit_bytes=40 * 1024 * 1024
             ),
-        )(in_flight, phase_index, absorption, jnp.asarray(high), jnp.asarray(low))
+        )(*[pltpu.with_memory_space_constraint(v, pltpu.HBM) for v in (in_flight, phase_index, absorption, jnp.asarray(high), jnp.asarray(low))])
 
     placed = (P("depth", None, "rows", None), P("depth", "rows", None), P("depth", "rows", None))
     return jax.shard_map(

time: 48.5 us -> 44.7 us (0.922)
  Pallas kernels: 46.6 us -> 43.8 us
  local copies, waits for them, and re-layouts: 1.67 us -> 0.71 us
    pallas_call x1, Pallas kernels: 46.6 us -> 43.8 us  [local(): pl.pallas_call(functools.partial(kernel, groups, rows, PLANE_WIDTH), out_...]
    unnamed x1, local copies, waits for them, and re-layouts: 1.67 us -> 0.71 us
where the time goes in v2:
time: 44.7 us; the launch traced here: 44.6 us
  Pallas kernels  43.8 us (98%)
  local copies, waits for them, and re-layouts  0.71 us (2%)
    pallas_call x1, Pallas kernels, local(): pl.pallas_call(functools.partial(kernel, groups, rows, PLANE_WIDTH), out_...  43.8 us

profile of v2, /device:TPU:6, one launch (start us, length us, event | category | flops | bytes accessed | tf_op | source)
XLA Modules:
  0.0 44.6 jit_solution(17934086909394028314)
XLA Ops:
  0.0 43.8 %shard_map.55 = f32[1,2,32,1024]{3,2,1,0:T(8,128)S(1)} custom-call(f32[1,2,32,1024]{3,2,1,0:T(8,128)} %field_hbm.1, bf16[2,32,1024]{2,1,0:T(8,128)(2,1)} %index_hbm.1, bf16[2,32,1024]{2,1,0:T(8,128)(2,1)} %loss_hbm.1, bf16[8,256,256]{2,1,0:T(8,128)(2,1)} %constant.4.clone.high_hbm, bf16[8,256,256]{2,1,0:T(8,128)(2,1)} %constant.5.clone.low_hbm), custom_call_target="tpu_custom_call" | custom-call | tf_op jit(solution)/shard_map/pallas_call | solution.py:436
  43.9 0.7 %copy.7 = f32[1,2,32,1024]{3,2,1,0:T(8,128)} copy(f32[1,2,32,1024]{3,2,1,0:T(8,128)S(1)} %shard_map.55) | data formatting | bytes 524288

commit v3 on v2

--- a/solution.py
+++ b/solution.py
@@ -138,7 +138,6 @@
     row_tall = lax.broadcasted_iota(jnp.int32, (tall, LANES), 0)
     outside = ((row_tall < HALO) & (me == 0)) | ((row_tall >= HALO + slab) & (me == rows - 1))
     lat = jnp.where(outside, 0.0, lateral)
-    lat_slab = jnp.full((slab, LANES), lateral, jnp.float32)
 
     for slot in range(2):
         for part in range(2):
@@ -200,8 +199,8 @@
 
     def put_coefficients(tick, a, values):
         for k in range(SLICES):
-            coef[tick, k, a, HALO : HALO + slab] = contrast * values[k] - 4.0 * lat_slab
-            damp[tick, k, a, HALO : HALO + slab] = contrast * values[SLICES + k]
+            coef[tick, k, a, HALO : HALO + slab] = (contrast / lateral) * values[k] - 4.0
+            damp[tick, k, a, HALO : HALO + slab] = (contrast / lateral) * values[SLICES + k]
 
     def put_spec_edges(a, values):
         for kind in range(2):
@@ -215,13 +214,12 @@
         for side, start in ((0, 0), (1, HALO + slab)):
             off = (me == 0) if side == 0 else (me == rows - 1)
             keep = jnp.where(off, 0.0, 1.0)
-            lat_here = lateral * keep
             for a in range(tiles):
                 for part in range(2) if field_of else ():
                     term[0, part, a, HALO + start : 2 * HALO + start] = field_of(side, part, a) * keep
                 for k in range(SLICES):
-                    coef[tick, k, a, start : start + HALO] = contrast * spec_of(side, 0, k, a) - 4.0 * lat_here
-                    damp[tick, k, a, start : start + HALO] = contrast * spec_of(side, 1, k, a)
+                    coef[tick, k, a, start : start + HALO] = (contrast / lateral) * spec_of(side, 0, k, a) - 4.0
+                    damp[tick, k, a, start : start + HALO] = (contrast / lateral) * spec_of(side, 1, k, a)
 
     lane_chunk = lax.broadcasted_iota(jnp.int32, (CHUNK, LANES), 1)
     first_lane = lane_chunk == 0
@@ -235,6 +233,7 @@
         for r in range(HALO if final else 0, HALO + slab if final else tall, CHUNK):
             at = slice(r, r + CHUNK)
             lo, hi = HALO + r, HALO + r + CHUNK
+            plus, minus = lat[at] * scale, lat[at] * (-scale)
 
             def fetch(a):
                 if a < 0 or a >= tiles:
@@ -250,11 +249,11 @@
                     west = jnp.where(first_lane, before[part][1], here[part][1])
                     east = jnp.where(last_lane, after[part][2], here[part][2])
                     beside = term[src, part, a, lo - 1 : hi - 1] + term[src, part, a, lo + 1 : hi + 1]
-                    stirred.append(lat[at] * (beside + (west + east)) + coef[tick, k, a, at] * here[part][0])
+                    stirred.append((beside + (west + east)) + coef[tick, k, a, at] * here[part][0])
                 loss = damp[tick, k, a, at]
                 new = [
-                    (stirred[1] + loss * here[0][0]) * (-scale),
-                    (stirred[0] - loss * here[1][0]) * scale,
+                    (stirred[1] + loss * here[0][0]) * minus,
+                    (stirred[0] - loss * here[1][0]) * plus,
                 ]
                 for part in range(2):
                     so_far = here[part][0] if degree == 1 else total[part, a, at]

time: 44.7 us -> 44.7 us (level)
  no operation moved by 1% of the time
where the time goes in v3:
time: 44.7 us; the launch traced here: 44.6 us
  Pallas kernels  43.8 us (98%)
  local copies, waits for them, and re-layouts  0.71 us (2%)
    pallas_call x1, Pallas kernels, local(): pl.pallas_call(functools.partial(kernel, groups, rows, PLANE_WIDTH), out_...  43.8 us

profile of v3, /device:TPU:6, one launch (start us, length us, event | category | flops | bytes accessed | tf_op | source)
XLA Modules:
  0.0 44.6 jit_solution(4200921105960788259)
XLA Ops:
  0.0 43.8 %shard_map.55 = f32[1,2,32,1024]{3,2,1,0:T(8,128)S(1)} custom-call(f32[1,2,32,1024]{3,2,1,0:T(8,128)} %field_hbm.1, bf16[2,32,1024]{2,1,0:T(8,128)(2,1)} %index_hbm.1, bf16[2,32,1024]{2,1,0:T(8,128)(2,1)} %loss_hbm.1, bf16[8,256,256]{2,1,0:T(8,128)(2,1)} %constant.4.clone.high_hbm, bf16[8,256,256]{2,1,0:T(8,128)(2,1)} %constant.5.clone.low_hbm), custom_call_target="tpu_custom_call" | custom-call | tf_op jit(solution)/shard_map/pallas_call | solution.py:435
  43.8 0.7 %copy.7 = f32[1,2,32,1024]{3,2,1,0:T(8,128)} copy(f32[1,2,32,1024]{3,2,1,0:T(8,128)S(1)} %shard_map.55) | data formatting | bytes 524288

commit v4 on v2

--- a/solution.py
+++ b/solution.py
@@ -183,7 +183,7 @@
                         device_id=(depth, target), device_id_type=MESH,
                     )
                 )
-        return copies
+        return copies[0::3] + copies[1::3] + copies[2::3]
 
     def halo_copies(src, dst, kind):
         copies = []

time: 44.7 us -> 44.7 us (level)
  no operation moved by 1% of the time
where the time goes in v4:
time: 44.7 us; the launch traced here: 44.6 us
  Pallas kernels  43.8 us (98%)
  local copies, waits for them, and re-layouts  0.71 us (2%)
    pallas_call x1, Pallas kernels, local(): pl.pallas_call(functools.partial(kernel, groups, rows, PLANE_WIDTH), out_...  43.8 us

profile of v4, /device:TPU:6, one launch (start us, length us, event | category | flops | bytes accessed | tf_op | source)
XLA Modules:
  0.0 44.6 jit_solution(18203852172492697144)
XLA Ops:
  0.0 43.8 %shard_map.55 = f32[1,2,32,1024]{3,2,1,0:T(8,128)S(1)} custom-call(f32[1,2,32,1024]{3,2,1,0:T(8,128)} %field_hbm.1, bf16[2,32,1024]{2,1,0:T(8,128)(2,1)} %index_hbm.1, bf16[2,32,1024]{2,1,0:T(8,128)(2,1)} %loss_hbm.1, bf16[8,256,256]{2,1,0:T(8,128)(2,1)} %constant.4.clone.high_hbm, bf16[8,256,256]{2,1,0:T(8,128)(2,1)} %constant.5.clone.low_hbm), custom_call_target="tpu_custom_call" | custom-call | tf_op jit(solution)/shard_map/pallas_call | solution.py:436
  43.9 0.7 %copy.7 = f32[1,2,32,1024]{3,2,1,0:T(8,128)} copy(f32[1,2,32,1024]{3,2,1,0:T(8,128)S(1)} %shard_map.55) | data formatting | bytes 524288
